TPU v7x, 32 devices: a whole 2x2x4 slice. The times are simulated.
32 devices in a mesh: fsdp: 8 (over y, x, core), tp: 4 (over z).
Axes of the slice: x: 2, y: 2, z: 4, core: 2. Of those that a mesh axis runs over, the one named last changes fastest.
Arguments:
- features: bfloat16 [1024, 8192], P('fsdp'), may hold values from -17 to 17
- key_partials: bfloat16 [1024, 4, 128], P('fsdp', 'tp'), may hold values from -0.30935922 to 0.30935922
- momentum: float32 [4096, 4, 128], P('fsdp', 'tp'), may hold values from -6 to 6
Outputs:
- update: float32 [4096, 4, 128], P('fsdp', 'tp')
- new_momentum: float32 [4096, 4, 128], P('fsdp', 'tp')
All inputs are finite; a program needn't handle non-finite values.
Results may differ from a plain program's by a relative error of at most 0.0003.
Values may be sent and summed in bfloat16 or wider, within the bound.
No kernel may reach another device: no remote copies, remote signals or barrier semaphores. Data moves between devices by JAX's collectives and lax.ppermute only.
A program may use at most 64 MiB of HBM per device.

v0:
```python
import math
import jax
import jax.numpy as jnp
from jax import lax
from jax.sharding import PartitionSpec as P

D_W = 8192
ITERS = 5
retain = 0.95
first_coef = 3.4445
second_coef = -4.775
third_coef = 2.0315
epsilon = 1e-07
shrink = 0.2


def swapped(block, axis, distance):
    count = lax.axis_size(axis)
    route = []
    for low in range(count):
        high = low | 1 << distance
        if high != low and high < count:
            route += [(low, high), (high, low)]
    return lax.ppermute(block, axis, route)


def on_device(features, key_partials, momentum):
    precise = lax.Precision.HIGHEST
    contract = (((0,), (0,)), ((), ()))
    parity = lax.axis_index("tp") % 2
    own_part = key_partials[:, 0, :]
    head_size = key_partials.shape[2]
    rows_half = momentum.shape[0]
    shard = lax.psum_scatter(
        lax.dot_general(features, own_part, contract, preferred_element_type=jnp.float32),
        "fsdp",
        scatter_dimension=0,
        tiled=True,
    )
    pieces = shard.reshape(2, rows_half, head_size)
    mine = jnp.where(parity == 0, pieces[0], pieces[1])
    other = jnp.where(parity == 0, pieces[1], pieces[0])
    grads = mine + swapped(other, "tp", 0)
    moment = momentum[:, 0, :]
    fresh = retain * moment + grads
    blend = grads + retain * fresh
    gram = lax.dot_general(blend, blend, contract, precision=precise)
    gram = lax.psum(gram, "fsdp")
    gram = gram + swapped(gram, "tp", 0)
    inverse = 1.0 / (jnp.sqrt(jnp.trace(gram)) + epsilon)
    state = blend * inverse
    gram = gram * (inverse * inverse)
    identity = jnp.eye(head_size, dtype=jnp.float32)
    for step in range(ITERS):
        square = jnp.dot(gram, gram, precision=precise)
        poly = first_coef * identity + second_coef * gram + third_coef * square
        state = jnp.dot(state, poly, precision=precise)
        gram = jnp.dot(poly, jnp.dot(gram, poly, precision=precise), precision=precise)
    update = shrink * math.sqrt(D_W) * state
    return (update[:, None, :], fresh[:, None, :])


def solution(mesh):
    placed = (P("fsdp", None), P("fsdp", "tp", None), P("fsdp", "tp", None))
    return jax.shard_map(
        on_device,
        mesh=mesh,
        in_specs=placed,
        out_specs=(P("fsdp", "tp", None), P("fsdp", "tp", None)),
        check_vma=False,
    )
```

profile of v0, /device:TPU:0, one launch (start us, length us, event | category | flops | bytes accessed | tf_op | source)
XLA Modules:
  0.0 150.5 jit_solution(14905172062143592151)
XLA Ops:
  7.2 0.0 reduce-scatter.2.cloned.1.call-start
  7.2 1.5 %copy-done = bf16[128,8192]{1,0:T(8,128)(2,1)S(1)} copy-done((bf16[128,8192]{1,0:T(8,128)(2,1)S(1)}, bf16[128,8192]{1,0:T(8,128)(2,1)}, u32[]{:S(2)}) %copy-start) | copy-done | bytes 2097176
  8.8 3.4 %fusion.14 = f32[8192,128]{1,0:T(8,128)} fusion(bf16[128,8192]{1,0:T(8,128)(2,1)S(1)} %copy-done, bf16[128,1,128]{2,0,1:T(8,128)(2,1)} %param.4), kind=kOutput, calls=%fused_computation.29 | convolution fusion | flops 268435456 | bytes 6324224 | tf_op jit(solution)/shard_map/dot_general | solution.py:35
  12.2 0.0 all-reduce.2.cloned.1.call-start
  12.3 54.0 %reduce-scatter.2.cloned.1.call-done = f32[1024,128]{1,0:T(8,128)} async-done(((f32[8192,128]{1,0:T(8,128)}), f32[1024,128]{1,0:T(8,128)}) %reduce-scatter.2.cloned.1.call-update) | async-done | bytes 524304 | tf_op jit(solution)/shard_map/reduce_scatter | solution.py:34
  66.3 1.1 slice_select_fusion
  67.3 1.5 %collective-permute-start = (f32[512,128]{1,0:T(8,128)S(1)}, f32[512,128]{1,0:T(8,128)S(1)}, u32[]{:S(2)}, u32[]{:S(2)}) collective-permute-start(f32[512,128]{1,0:T(8,128)S(1)} %slice_select_fusion), channel_id=1, source_target_pairs={{0,1},{1,0},{2,3},{3,2},{4,5},{5,4},{6,7},{7,6},{8,9},{9,8},{10,11... | collective-permute-start | bytes 786440 | tf_op jit(solution)/shard_map/ppermute | solution.py:24
  68.9 6.4 %collective-permute-done = f32[512,128]{1,0:T(8,128)S(1)} collective-permute-done((f32[512,128]{1,0:T(8,128)S(1)}, f32[512,128]{1,0:T(8,128)S(1)}, u32[]{:S(2)}, u32[]{:S(2)}) %collective-permute-start) | collective-permute-done | bytes 262176 | tf_op jit(solution)/shard_map/ppermute | solution.py:24
  75.3 1.8 %bitcast_add_fusion = (f32[512,128]{1,0:T(8,128)}, f32[512,128]{1,0:T(8,128)S(1)}) fusion(f32[512,1,128]{2,0,1:T(8,128)S(1)} %bitcast.51, f32[512,128]{1,0:T(8,128)S(1)} %collective-permute-done, f32[1024,128]{1,0:T(8,128)} %reduce-scatter.2.cloned.1.call-done, pred[]{:T(512)S(6)} %eq.21), kind=kLoop, calls=%fused_computation.10 | loop fusion | flops 262144 | bytes 1572865 | tf_op jit(solution)/shard_map/add | solution.py:45
  77.1 1.2 fusion.7
  78.3 53.3 %all-reduce.2.cloned.1.call-done = f32[128,128]{1,0:T(8,128)} async-done(((f32[128,128]{1,0:T(8,128)}), f32[128,128]{1,0:T(8,128)}) %all-reduce.2.cloned.1.call-update) | async-done | bytes 65552 | tf_op jit(solution)/shard_map/psum | solution.py:48
  131.7 1.5 collective-permute-start.1
  133.2 3.0 %collective-permute-done.1 = f32[128,128]{1,0:T(8,128)S(1)} collective-permute-done((f32[128,128]{1,0:T(8,128)}, f32[128,128]{1,0:T(8,128)S(1)}, u32[]{:S(2)}, u32[]{:S(2)}) %collective-permute-start.1) | collective-permute-done | bytes 65568 | tf_op jit(solution)/shard_map/ppermute | solution.py:24
  136.2 1.5 select_reduce_fusion
  138.4 0.2 fusion.8
  138.6 0.4 fusion.4
  139.0 0.2 fusion.9
  139.2 0.2 fusion.20
  139.4 0.2 fusion.3
  139.6 0.2 fusion.22
  139.8 0.4 fusion.21
  140.2 0.2 fusion.23
  140.4 0.2 fusion.2
  140.6 0.2 fusion.25
  140.8 0.4 fusion.24
  141.2 0.2 fusion.26
  141.4 0.2 fusion.1
  141.6 0.2 fusion.28
  141.8 0.4 fusion.27
  142.2 0.2 fusion.29
  142.4 0.2 fusion
  142.6 1.1 convolution_multiply_fusion
  (5 shorter events, 0.0 us)
Async XLA Ops:
  7.2 1.6 %copy-start = (bf16[128,8192]{1,0:T(8,128)(2,1)S(1)}, bf16[128,8192]{1,0:T(8,128)(2,1)}, u32[]{:S(2)}) copy-start(bf16[128,8192]{1,0:T(8,128)(2,1)} %param.3) | copy-start | bytes 6291460
  7.2 59.1 %reduce-scatter.2.cloned.1.call-start = ((), (), s32[]{:S(2)}) async-start(), calls=%async_computation.1 | async-start | bytes 4718592 | tf_op jit(solution)/shard_map/reduce_scatter | solution.py:34
  12.2 63.1 %copy-start.1 = (f32[512,1,128]{2,1,0:T(1,128)S(1)}, f32[512,1,128]{2,1,0:T(1,128)}, u32[]{:S(2)}) copy-start(f32[512,1,128]{2,1,0:T(1,128)} %param.5) | copy-start | bytes 786436
  12.2 119.5 %all-reduce.2.cloned.1.call-start = ((), (), s32[]{:S(2)}) async-start(), calls=%async_computation.2 | async-start | bytes 131072 | tf_op jit(solution)/shard_map/psum | solution.py:48
  67.3 7.9 %collective-permute-start = (f32[512,128]{1,0:T(8,128)S(1)}, f32[512,128]{1,0:T(8,128)S(1)}, u32[]{:S(2)}, u32[]{:S(2)}) collective-permute-start(f32[512,128]{1,0:T(8,128)S(1)} %slice_select_fusion), channel_id=1, source_target_pairs={{0,1},{1,0},{2,3},{3,2},{4,5},{5,4},{6,7},{7,6},{8,9},{9,8},{10,11... | collective-permute-start | bytes 786440 | tf_op jit(solution)/shard_map/ppermute | solution.py:24
  131.7 4.5 %collective-permute-start.1 = (f32[128,128]{1,0:T(8,128)}, f32[128,128]{1,0:T(8,128)S(1)}, u32[]{:S(2)}, u32[]{:S(2)}) collective-permute-start(f32[128,128]{1,0:T(8,128)} %all-reduce.2.cloned.1.call-done), channel_id=1, source_target_pairs={{0,1},{1,0},{2,3},{3,2},{4,5},{5,4},{6,7},{7,6},{8,9},{9,8},{10,11... | collective-permute-start | bytes 196616 | tf_op jit(solution)/shard_map/ppermute | solution.py:24
Sparse Core Ops, SparseCore 0:
  12.4 53.8 reduce-scatter.1
  78.5 53.1 all-reduce.1
where the time goes:
time: 151 us
  waiting for transfers between devices  117 us (77%)
  between operations  14.9 us (10%)
  matrix products  9.86 us (7%)
  other arithmetic  4.35 us (3%)
  starting transfers between devices  3.11 us (2%)
  local copies, waits for them, and re-layouts  1.55 us (1%)
    reduce_scatter x1, waiting for transfers between devices, on_device(): lax.psum_scatter(lax.dot_general(features, own_part, contract, preferred_...  54 us
    psum x1, waiting for transfers between devices, on_device(): gram = lax.psum(gram, 'fsdp')  53.3 us
    ppermute x2, waiting for transfers between devices, swapped(): return lax.ppermute(block, axis, route)  9.37 us
    dot_general x1, matrix products, on_device(): lax.dot_general(features, own_part, contract, preferred_element_type=jnp....  3.45 us
    ppermute x2, starting transfers between devices, swapped(): return lax.ppermute(block, axis, route)  3.03 us
  transfers between devices with their start and end apart: 4, of which 4 were waited for; matrix products, arithmetic and copies ran while one was open for 0% of the time, Pallas kernels for 0%

commit v1 on v0

--- a/solution.py
+++ b/solution.py
@@ -1,3 +1,4 @@
+import functools
 import math
 import jax
 import jax.numpy as jnp
@@ -12,6 +13,18 @@
 third_coef = 2.0315
 epsilon = 1e-07
 shrink = 0.2
+
+
+def measure_halves(raw, device_axis):
+    total_devices = lax.axis_size(device_axis)
+    raw_out = lambda small: [(b, b ^ small) for b in range(total_devices)]
+    x_new = raw
+    for jj in range(total_devices.bit_length() - 1):
+        x_new = x_new + lax.ppermute(x_new, axis_name=device_axis, perm=raw_out(1 << jj))
+    return x_new
+
+
+replace_counts_up = functools.partial(measure_halves, device_axis="fsdp")
 
 
 def swapped(block, axis, distance):
@@ -45,7 +58,7 @@
     fresh = retain * moment + grads
     blend = grads + retain * fresh
     gram = lax.dot_general(blend, blend, contract, precision=precise)
-    gram = lax.psum(gram, "fsdp")
+    gram = replace_counts_up(gram)
     gram = gram + swapped(gram, "tp", 0)
     inverse = 1.0 / (jnp.sqrt(jnp.trace(gram)) + epsilon)
     state = blend * inverse

time: 151 us -> 106 us (0.70)
  waiting for transfers between devices: 117 us -> 70 us
  starting transfers between devices: 3.11 us -> 6.29 us
    psum x1 -> x0, waiting for transfers between devices: 53.3 us -> none  [on_device(): gram = lax.psum(gram, 'fsdp')]
    ppermute x0 -> x3, waiting for transfers between devices: none -> 6.83 us  [measure_halves(): lax.ppermute(x_new, axis_name=device_axis, perm=raw_out(1 << jj))]
    ppermute x0 -> x3, starting transfers between devices: none -> 3.14 us  [measure_halves(): lax.ppermute(x_new, axis_name=device_axis, perm=raw_out(1 << jj))]
  transfers between devices with their start and end apart: 4 -> 6, of which waited for: 4 -> 6; matrix products, arithmetic and copies ran while one was open for 0% -> 0% of each run, Pallas kernels for 0% -> 0%
where the time goes in v1:
time: 106 us
  waiting for transfers between devices  70 us (66%)
  between operations  14.9 us (14%)
  matrix products  9.22 us (9%)
  starting transfers between devices  6.29 us (6%)
  other arithmetic  3.52 us (3%)
  local copies, waits for them, and re-layouts  1.55 us (1%)
    reduce_scatter x1, waiting for transfers between devices, on_device(): lax.psum_scatter(lax.dot_general(features, own_part, contract, preferred_...  54 us
    ppermute x2, waiting for transfers between devices, swapped(): return lax.ppermute(block, axis, route)  9.15 us
    ppermute x3, waiting for transfers between devices, measure_halves(): lax.ppermute(x_new, axis_name=device_axis, perm=raw_out(1 << jj))  6.83 us
    dot_general x1, matrix products, on_device(): lax.dot_general(features, own_part, contract, preferred_element_type=jnp....  3.45 us
    ppermute x3, starting transfers between devices, measure_halves(): lax.ppermute(x_new, axis_name=device_axis, perm=raw_out(1 << jj))  3.14 us
    ppermute x2, starting transfers between devices, swapped(): return lax.ppermute(block, axis, route)  3.11 us
    dot_general x5, matrix products, on_device(): state = jnp.dot(state, poly, precision=precise)  2.52 us
  transfers between devices with their start and end apart: 6, of which 6 were waited for; matrix products, arithmetic and copies ran while one was open for 0% of the time, Pallas kernels for 0%

profile of v1, /device:TPU:0, one launch (start us, length us, event | category | flops | bytes accessed | tf_op | source)
XLA Modules:
  0.0 105.5 jit_solution(10594878731344504261)
XLA Ops:
  7.2 1.5 %copy-done = bf16[128,8192]{1,0:T(8,128)(2,1)S(1)} copy-done((bf16[128,8192]{1,0:T(8,128)(2,1)S(1)}, bf16[128,8192]{1,0:T(8,128)(2,1)}, u32[]{:S(2)}) %copy-start) | copy-done | bytes 2097176
  8.8 3.5 %fusion.14 = f32[8192,128]{1,0:T(8,128)} fusion(bf16[128,8192]{1,0:T(8,128)(2,1)S(1)} %copy-done, bf16[128,1,128]{2,0,1:T(8,128)(2,1)} %param.4), kind=kOutput, calls=%fused_computation.29 | convolution fusion | flops 268435456 | bytes 6324224 | tf_op jit(solution)/shard_map/dot_general | solution.py:48
  12.3 54.0 %reduce-scatter.2.cloned.1.call-done = f32[1024,128]{1,0:T(8,128)} async-done(((f32[8192,128]{1,0:T(8,128)}), f32[1024,128]{1,0:T(8,128)}) %reduce-scatter.2.cloned.1.call-update) | async-done | bytes 524304 | tf_op jit(solution)/shard_map/reduce_scatter | solution.py:47
  66.3 1.1 %slice_select_fusion = f32[512,128]{1,0:T(8,128)S(1)} fusion(f32[1024,128]{1,0:T(8,128)} %reduce-scatter.2.cloned.1.call-done, pred[]{:T(512)S(6)} %eq.21), kind=kLoop, calls=%fused_computation.15 | loop fusion | flops 65536 | bytes 786433 | tf_op jit(solution)/shard_map/jit(_where)/select_n | solution.py:55
  67.3 1.5 %collective-permute-start = (f32[512,128]{1,0:T(8,128)S(1)}, f32[512,128]{1,0:T(8,128)S(1)}, u32[]{:S(2)}, u32[]{:S(2)}) collective-permute-start(f32[512,128]{1,0:T(8,128)S(1)} %slice_select_fusion), channel_id=1, source_target_pairs={{0,1},{1,0},{2,3},{3,2},{4,5},{5,4},{6,7},{7,6},{8,9},{9,8},{10,11... | collective-permute-start | bytes 786440 | tf_op jit(solution)/shard_map/ppermute | solution.py:37
  68.9 6.4 %collective-permute-done = f32[512,128]{1,0:T(8,128)S(1)} collective-permute-done((f32[512,128]{1,0:T(8,128)S(1)}, f32[512,128]{1,0:T(8,128)S(1)}, u32[]{:S(2)}, u32[]{:S(2)}) %collective-permute-start) | collective-permute-done | bytes 262176 | tf_op jit(solution)/shard_map/ppermute | solution.py:37
  75.3 1.8 %bitcast_add_fusion = (f32[512,128]{1,0:T(8,128)}, f32[512,128]{1,0:T(8,128)S(1)}) fusion(f32[512,1,128]{2,0,1:T(8,128)S(1)} %bitcast.51, f32[512,128]{1,0:T(8,128)S(1)} %collective-permute-done, f32[1024,128]{1,0:T(8,128)} %reduce-scatter.2.cloned.1.call-done, pred[]{:T(512)S(6)} %eq.21), kind=kLoop, calls=%fused_computation.10 | loop fusion | flops 262144 | bytes 1572865 | tf_op jit(solution)/shard_map/add | solution.py:58
  77.1 0.6 fusion.7
  77.8 1.2 %collective-permute-done.1 = f32[128,128]{1,0:T(8,128)S(1)} collective-permute-done((f32[128,128]{1,0:T(8,128)S(1)}, f32[128,128]{1,0:T(8,128)S(1)}, u32[]{:S(2)}, u32[]{:S(2)}) %collective-permute-start.1) | collective-permute-done | bytes 65568 | tf_op jit(solution)/shard_map/ppermute | solution.py:23
  79.0 1.5 %collective-permute-start.2 = (f32[128,128]{1,0:T(8,128)S(1)}, f32[128,128]{1,0:T(8,128)S(1)}, u32[]{:S(2)}, u32[]{:S(2)}) collective-permute-start(f32[128,128]{1,0:T(8,128)S(1)} %add.64), channel_id=1, source_target_pairs={{0,8},{4,12},{8,0},{12,4},{16,24},{20,28},{24,16},{28,20},{1,9},{5... | collective-permute-start | bytes 196616 | tf_op jit(solution)/shard_map/ppermute | solution.py:23
  80.6 2.8 %collective-permute-done.2 = f32[128,128]{1,0:T(8,128)S(1)} collective-permute-done((f32[128,128]{1,0:T(8,128)S(1)}, f32[128,128]{1,0:T(8,128)S(1)}, u32[]{:S(2)}, u32[]{:S(2)}) %collective-permute-start.2) | collective-permute-done | bytes 65568 | tf_op jit(solution)/shard_map/ppermute | solution.py:23
  83.4 1.5 %collective-permute-start.3 = (f32[128,128]{1,0:T(8,128)S(1)}, f32[128,128]{1,0:T(8,128)S(1)}, u32[]{:S(2)}, u32[]{:S(2)}) collective-permute-start(f32[128,128]{1,0:T(8,128)S(1)} %add.65), channel_id=1, source_target_pairs={{0,16},{4,20},{8,24},{12,28},{16,0},{20,4},{24,8},{28,12},{1,17},{... | collective-permute-start | bytes 196616 | tf_op jit(solution)/shard_map/ppermute | solution.py:23
  84.9 2.8 %collective-permute-done.3 = f32[128,128]{1,0:T(8,128)S(1)} collective-permute-done((f32[128,128]{1,0:T(8,128)S(1)}, f32[128,128]{1,0:T(8,128)S(1)}, u32[]{:S(2)}, u32[]{:S(2)}) %collective-permute-start.3) | collective-permute-done | bytes 65568 | tf_op jit(solution)/shard_map/ppermute | solution.py:23
  87.7 1.6 %collective-permute-start.4 = (f32[128,128]{1,0:T(8,128)S(1)}, f32[128,128]{1,0:T(8,128)S(1)}, u32[]{:S(2)}, u32[]{:S(2)}) collective-permute-start(f32[128,128]{1,0:T(8,128)S(1)} %add.66), channel_id=1, source_target_pairs={{0,1},{1,0},{2,3},{3,2},{4,5},{5,4},{6,7},{7,6},{8,9},{9,8},{10,11... | collective-permute-start | bytes 196616 | tf_op jit(solution)/shard_map/ppermute | solution.py:37
  89.3 2.8 %collective-permute-done.4 = f32[128,128]{1,0:T(8,128)S(1)} collective-permute-done((f32[128,128]{1,0:T(8,128)S(1)}, f32[128,128]{1,0:T(8,128)S(1)}, u32[]{:S(2)}, u32[]{:S(2)}) %collective-permute-start.4) | collective-permute-done | bytes 65568 | tf_op jit(solution)/shard_map/ppermute | solution.py:37
  92.0 0.6 select_reduce_fusion
  93.4 0.2 fusion.8
  93.6 0.4 fusion.4
  94.0 0.2 fusion.9
  94.2 0.2 fusion.20
  94.4 0.2 fusion.3
  94.8 0.4 fusion.21
  95.2 0.2 fusion.23
  95.4 0.2 fusion.2
  95.6 0.2 fusion.25
  95.8 0.4 fusion.24
  96.2 0.2 fusion.26
  96.4 0.2 fusion.1
  96.8 0.4 fusion.27
  97.2 0.2 fusion.29
  97.4 0.2 fusion
  97.6 1.1 %convolution_multiply_fusion = f32[512,128]{1,0:T(8,128)} fusion(f32[512,128]{1,0:T(8,128)S(1)} %fusion.27, f32[128,128]{1,0:T(8,128)S(1)} %fusion), kind=kOutput, calls=%fused_computation | convolution fusion | flops 100728832 | bytes 589824 | tf_op jit(solution)/shard_map/dot_general | solution.py:70
  (11 shorter events, 0.6 us)
Async XLA Ops:
  7.2 1.6 %copy-start = (bf16[128,8192]{1,0:T(8,128)(2,1)S(1)}, bf16[128,8192]{1,0:T(8,128)(2,1)}, u32[]{:S(2)}) copy-start(bf16[128,8192]{1,0:T(8,128)(2,1)} %param.3) | copy-start | bytes 6291460
  7.2 59.1 %reduce-scatter.2.cloned.1.call-start = ((), (), s32[]{:S(2)}) async-start(), calls=%async_computation.1 | async-start | bytes 4718592 | tf_op jit(solution)/shard_map/reduce_scatter | solution.py:47
  12.2 63.1 %copy-start.1 = (f32[512,1,128]{2,1,0:T(1,128)S(1)}, f32[512,1,128]{2,1,0:T(1,128)}, u32[]{:S(2)}) copy-start(f32[512,1,128]{2,1,0:T(1,128)} %param.5) | copy-start | bytes 786436
  67.3 7.9 %collective-permute-start = (f32[512,128]{1,0:T(8,128)S(1)}, f32[512,128]{1,0:T(8,128)S(1)}, u32[]{:S(2)}, u32[]{:S(2)}) collective-permute-start(f32[512,128]{1,0:T(8,128)S(1)} %slice_select_fusion), channel_id=1, source_target_pairs={{0,1},{1,0},{2,3},{3,2},{4,5},{5,4},{6,7},{7,6},{8,9},{9,8},{10,11... | collective-permute-start | bytes 786440 | tf_op jit(solution)/shard_map/ppermute | solution.py:37
  77.7 1.3 %collective-permute-start.1 = (f32[128,128]{1,0:T(8,128)S(1)}, f32[128,128]{1,0:T(8,128)S(1)}, u32[]{:S(2)}, u32[]{:S(2)}) collective-permute-start(f32[128,128]{1,0:T(8,128)S(1)} %fusion.7), channel_id=1, source_target_pairs={{0,4},{4,0},{8,12},{12,8},{16,20},{20,16},{24,28},{28,24},{1,5},{5... | collective-permute-start | bytes 196616 | tf_op jit(solution)/shard_map/ppermute | solution.py:23
  79.0 4.3 %collective-permute-start.2 = (f32[128,128]{1,0:T(8,128)S(1)}, f32[128,128]{1,0:T(8,128)S(1)}, u32[]{:S(2)}, u32[]{:S(2)}) collective-permute-start(f32[128,128]{1,0:T(8,128)S(1)} %add.64), channel_id=1, source_target_pairs={{0,8},{4,12},{8,0},{12,4},{16,24},{20,28},{24,16},{28,20},{1,9},{5... | collective-permute-start | bytes 196616 | tf_op jit(solution)/shard_map/ppermute | solution.py:23
  83.4 4.3 %collective-permute-start.3 = (f32[128,128]{1,0:T(8,128)S(1)}, f32[128,128]{1,0:T(8,128)S(1)}, u32[]{:S(2)}, u32[]{:S(2)}) collective-permute-start(f32[128,128]{1,0:T(8,128)S(1)} %add.65), channel_id=1, source_target_pairs={{0,16},{4,20},{8,24},{12,28},{16,0},{20,4},{24,8},{28,12},{1,17},{... | collective-permute-start | bytes 196616 | tf_op jit(solution)/shard_map/ppermute | solution.py:23
  87.7 4.3 %collective-permute-start.4 = (f32[128,128]{1,0:T(8,128)S(1)}, f32[128,128]{1,0:T(8,128)S(1)}, u32[]{:S(2)}, u32[]{:S(2)}) collective-permute-start(f32[128,128]{1,0:T(8,128)S(1)} %add.66), channel_id=1, source_target_pairs={{0,1},{1,0},{2,3},{3,2},{4,5},{5,4},{6,7},{7,6},{8,9},{9,8},{10,11... | collective-permute-start | bytes 196616 | tf_op jit(solution)/shard_map/ppermute | solution.py:37
Sparse Core Ops, SparseCore 0:
  12.4 53.8 reduce-scatter.1
